TPU v7x, 32 devices: a whole 2x2x4 slice. The times are simulated.
32 devices in a mesh: dp: 2 (over core), row: 4 (over z), col: 4 (over y, x).
Axes of the slice: x: 2, y: 2, z: 4, core: 2. Of those that a mesh axis runs over, the one named last changes fastest.
Arguments:
- inputs: bfloat16 [512, 12288], P('dp', 'col'), may hold values from -6 to 6
- weight_tiles: bfloat16 [4, 4, 432, 4096], P('row', 'col', 'dp'), may hold values from -0.109375 to 0.109375
- tile_rows: int32 [4, 4, 432], P('row', 'col'), may hold values from 0 to 191, as said below
- tile_cols: int32 [4, 4, 432], P('row', 'col'), may hold values from 0 to 47, as said below
- tile_counts: int32 [4, 4], P('row', 'col'), may hold values from 54 to 432, as said below
- act_grad: bfloat16 [512, 49152], P('dp', ('row', 'col')), may hold values from -6 to 6
Outputs:
- activation: bfloat16 [512, 49152], P('dp', ('row', 'col'))
- input_grad: bfloat16 [512, 12288], P(('dp', 'row'), 'col')
- tile_grads: bfloat16 [4, 4, 432, 4096], P('row', 'col', 'dp')
Inputs may be any that keep to these rules, and one draw needn't show every extreme that they name: `tile_rows`: block row of a slot within its region; within each region the slots name distinct blocks. `tile_cols`: block column of a slot within its region. `tile_counts`: live slots of a region are its first ones; some region has all 432 slots live.
All inputs are finite; a program needn't handle non-finite values.
Results may differ from a plain program's by a relative error of at most 0.015.
Values may be sent and summed in bfloat16 or wider, within the bound.
No kernel may reach another device: no remote copies, remote signals or barrier semaphores. Data moves between devices by JAX's collectives and lax.ppermute only.
A program may use at most 128 MiB of HBM per device.

v0:
```python
import jax
import jax.numpy as jnp
from jax import lax
from jax.sharding import PartitionSpec as P

COEFF = 0.7978845608028654
CUBIC = 0.044715


def gelu_value(values):
    return 0.5 * values * (1.0 + jnp.tanh(COEFF * (values + CUBIC * values * values * values)))


def gelu_slope(values):
    inner = jnp.tanh(COEFF * (values + CUBIC * values * values * values))
    return 0.5 * (1.0 + inner) + 0.5 * values * (1.0 - inner * inner) * COEFF * (
        1.0 + 3.0 * CUBIC * values * values
    )


def group_loop(slot_count, advance, initial, widest):
    group_width = max((divisor for divisor in range(1, widest + 1) if slot_count % divisor == 0))

    def looped(group_index, running):
        return advance(running, group_index * group_width, group_width)

    return lax.fori_loop(0, slot_count // group_width, looped, initial)


def one_hot_rows(block_ids, block_total):
    return (block_ids[:, None] == jnp.arange(block_total)[None, :]).astype(jnp.bfloat16)


def pick_blocks(table, block_ids):
    selector = one_hot_rows(block_ids, table.shape[0])
    flat = table.reshape(table.shape[0], table.shape[1] * table.shape[2])
    picked = jnp.dot(selector, flat, preferred_element_type=jnp.float32).astype(jnp.bfloat16)
    return picked.reshape(block_ids.shape[0], table.shape[1], table.shape[2])


def place_blocks(running, products, block_ids):
    selector = one_hot_rows(block_ids, running.shape[0])
    flat = products.reshape(products.shape[0], products.shape[1] * products.shape[2])
    upper = flat.astype(jnp.bfloat16)
    lower = (flat - upper.astype(jnp.float32)).astype(jnp.bfloat16)
    added = jnp.dot(selector.T, upper, preferred_element_type=jnp.float32)
    added = added + jnp.dot(selector.T, lower, preferred_element_type=jnp.float32)
    return running + added.reshape(running.shape)


def local(inputs, weight_tiles, tile_rows, tile_cols, tile_counts, act_grad):
    token_count = inputs.shape[0]
    in_blocks = inputs.shape[1] // 64
    col_devices = lax.axis_size("col")
    share = act_grad.shape[1]
    out_blocks = share * col_devices // 64
    max_slots = tile_rows.shape[2]
    row_ids = tile_rows.reshape(max_slots)
    col_ids = tile_cols.reshape(max_slots)
    alive = (jnp.arange(max_slots) < tile_counts.reshape(())).astype(jnp.float32)
    input_blocks = inputs.T.reshape(in_blocks, 64, token_count)

    def slot_info(slot_start, group_width):
        rows_here = lax.dynamic_slice_in_dim(row_ids, slot_start, group_width)
        cols_here = lax.dynamic_slice_in_dim(col_ids, slot_start, group_width)
        alive_here = lax.dynamic_slice_in_dim(alive, slot_start, group_width)
        return (rows_here, cols_here, alive_here)

    empty_rows = jnp.zeros((out_blocks, 64, token_count), jnp.float32)
    piece = lax.all_gather(weight_tiles, "dp", axis=2, tiled=True)
    start = jnp.int32(0)
    piece_slots = piece.shape[2]
    piece_tiles = piece.reshape(piece_slots, 64, 64)

    def advance(inner_total, first, group_width):
        group_tiles = lax.dynamic_slice_in_dim(piece_tiles, first, group_width, 0)
        rows_here, cols_here, alive_here = slot_info(start + first, group_width)
        gathered = pick_blocks(input_blocks, cols_here)
        products = jnp.einsum(
            "sik,skt->sit", group_tiles, gathered, preferred_element_type=jnp.float32
        )
        products = products * alive_here[:, None, None]
        return place_blocks(inner_total, products, rows_here)

    pre_partial = group_loop(piece_slots, advance, empty_rows, 144)
    pre_partial = pre_partial.reshape(out_blocks * 64, token_count)
    pre_share = (
        lax.psum_scatter(pre_partial.astype(jnp.bfloat16), "col", scatter_dimension=0, tiled=True)
        .astype(jnp.float32)
        .T
    )
    activation = gelu_value(pre_share).astype(jnp.bfloat16)
    grad_share = (act_grad.astype(jnp.float32) * gelu_slope(pre_share)).astype(jnp.bfloat16)
    grad_full = lax.all_gather(grad_share, "col", axis=1, tiled=True)
    grad_blocks = grad_full.T.reshape(out_blocks, 64, token_count)
    empty_cols = jnp.zeros((in_blocks, 64, token_count), jnp.float32)
    piece = lax.all_gather(weight_tiles, "dp", axis=2, tiled=True)
    backward_start = jnp.int32(0)
    piece_slots = piece.shape[2]
    backward_piece_tiles = piece.reshape(piece_slots, 64, 64)

    def advance(inner_total, first, group_width):
        group_tiles = lax.dynamic_slice_in_dim(backward_piece_tiles, first, group_width, 0)
        rows_here, cols_here, alive_here = slot_info(backward_start + first, group_width)
        gathered = pick_blocks(grad_blocks, rows_here)
        products = jnp.einsum(
            "sik,sit->skt", group_tiles, gathered, preferred_element_type=jnp.float32
        )
        products = products * alive_here[:, None, None]
        return place_blocks(inner_total, products, cols_here)

    input_partial = group_loop(piece_slots, advance, empty_cols, 144)
    input_partial = input_partial.reshape(in_blocks * 64, token_count)
    input_grad = (
        lax.psum_scatter(input_partial.astype(jnp.bfloat16), "row", scatter_dimension=1, tiled=True)
        .astype(jnp.float32)
        .T.astype(jnp.bfloat16)
    )
    stored_slots = max_slots // lax.axis_size("dp")

    def advance(buffer, first, group_width):
        rows_here, cols_here, alive_here = slot_info(first, group_width)
        grads_here = pick_blocks(grad_blocks, rows_here)
        inputs_here = pick_blocks(input_blocks, cols_here)
        products = jnp.einsum(
            "sit,skt->sik", grads_here, inputs_here, preferred_element_type=jnp.float32
        )
        products = (products * alive_here[:, None, None]).reshape(group_width, 4096)
        return lax.dynamic_update_slice_in_dim(buffer, products, first, 0)

    tile_sum = lax.psum_scatter(
        group_loop(
            lax.axis_size("dp") * stored_slots,
            advance,
            jnp.zeros((lax.axis_size("dp") * stored_slots, 4096), jnp.float32),
            48,
        ).astype(jnp.bfloat16),
        "dp",
        scatter_dimension=0,
        tiled=True,
    )
    tile_grads = tile_sum.reshape(1, 1, stored_slots, 4096)
    return (activation, input_grad, tile_grads)


def solution(mesh):
    return jax.shard_map(
        local,
        mesh=mesh,
        in_specs=(
            P("dp", "col"),
            P("row", "col", "dp", None),
            P("row", "col", None),
            P("row", "col", None),
            P("row", "col"),
            P("dp", ("row", "col")),
        ),
        out_specs=(P("dp", ("row", "col")), P(("dp", "row"), "col"), P("row", "col", "dp", None)),
        check_vma=False,
    )
```

profile of v0, /device:TPU:0, one launch (start us, length us, event | category | flops | bytes accessed | tf_op | source)
XLA Modules:
  0.0 620.6 jit_solution(8441548578228094327)
XLA Ops:
  11.2 13.8 %all-gather.3.cloned.1.call-done = bf16[1,1,432,4096]{3,2,1,0:T(8,128)(2,1)} async-done(((bf16[1,1,216,4096]{3,2,1,0:T(8,128)(2,1)}), bf16[1,1,432,4096]{3,2,1,0:T(8,128)(2,1)}) %all-gather.3.cloned.1.call-update) | async-done | bytes 3538960 | tf_op jit(solution)/shard_map/all_gather | solution.py:70
  25.0 6.4 %copy.22 = bf16[1,1,432,4096]{2,3,1,0:T(8,128)(2,1)} copy(bf16[1,1,432,4096]{3,2,1,0:T(8,128)(2,1)} %all-gather.3.cloned.1.call-done) | data formatting | bytes 7077888 | tf_op jit(solution)/shard_map/all_gather | solution.py:70
  31.4 220.8 %while.45 = (s32[]{:T(128)}, f32[192,64,256]{2,1,0:T(8,128)}, s32[432]{0:T(512)S(1)}, bf16[432,64,64]{0,2,1:T(8,128)(2,1)}, s32[432]{0:T(512)S(1)}, /*index=5*/b...) while((s32[]{:T(128)}, f32[192,64,256]{2,1,0:T(8,128)}, ...), condition=%wide.wide.region_1.0_spmd.clone, body=%wide.wide.region_0.0_spmd.clone.sunk | while | flops 2366436096 | bytes 200939408 | solution.py:27
  46.6 11.4 %copy.66 = f32[18,8,64,256]{3,1,2,0:T(8,128)} copy(f32[18,8,64,256]{3,2,1,0:T(8,128)S(1)} %bitcast.144) | data formatting | bytes 18874368 | tf_op jit(solution)/shard_map/while
  58.0 5.6 fusion.72
  63.6 13.7 %convolution_add_fusion.6 = f32[192,16384]{1,0:T(8,128)} fusion(f32[192,16384]{1,0:T(8,128)S(1)} %fusion.72, f32[144,16384]{1,0:T(8,128)} %bitcast.142, s32[144]{0:T(256)S(1)} %dynamic_slice.115), kind=kOutput, calls=%fused_computation.8.clone.clone.1 | convolution fusion | flops 918580224 | bytes 34603584 | tf_op jit(solution)/shard_map/while/body/eval_jaxpr/dot_general | solution.py:47
  77.4 13.8 %copy.67 = f32[24,8,64,256]{3,2,1,0:T(8,128)} copy(f32[24,8,64,256]{3,1,2,0:T(8,128)} %bitcast.143) | data formatting | bytes 25165824 | tf_op jit(solution)/shard_map/while
  91.2 11.8 %bitcast_add_fusion.6 = f32[192,64,256]{2,1,0:T(8,128)} fusion(f32[24,8,64,256]{3,2,1,0:T(8,128)} %copy.67, f32[192,64,256]{2,1,0:T(8,128)} %get-tuple-element.774, pred[]{:T(512)S(6)} %compare.8), kind=kLoop, calls=%fused_computation.10.clone.clone.1 | loop fusion | flops 6291456 | bytes 37748736 | tf_op jit(solution)/shard_map/while/body/eval_jaxpr/add | solution.py:48
  118.1 11.4 %copy.66 = f32[18,8,64,256]{3,1,2,0:T(8,128)} copy(f32[18,8,64,256]{3,2,1,0:T(8,128)S(1)} %bitcast.144) | data formatting | bytes 18874368 | tf_op jit(solution)/shard_map/while
  129.6 5.6 fusion.72
  135.2 13.7 %convolution_add_fusion.6 = f32[192,16384]{1,0:T(8,128)} fusion(f32[192,16384]{1,0:T(8,128)S(1)} %fusion.72, f32[144,16384]{1,0:T(8,128)} %bitcast.142, s32[144]{0:T(256)S(1)} %dynamic_slice.115), kind=kOutput, calls=%fused_computation.8.clone.clone.1 | convolution fusion | flops 918580224 | bytes 34603584 | tf_op jit(solution)/shard_map/while/body/eval_jaxpr/dot_general | solution.py:47
  148.9 13.8 %copy.67 = f32[24,8,64,256]{3,2,1,0:T(8,128)} copy(f32[24,8,64,256]{3,1,2,0:T(8,128)} %bitcast.143) | data formatting | bytes 25165824 | tf_op jit(solution)/shard_map/while
  162.8 14.7 %bitcast_add_fusion.6 = f32[192,64,256]{2,1,0:T(8,128)} fusion(f32[24,8,64,256]{3,2,1,0:T(8,128)} %copy.67, f32[192,64,256]{2,1,0:T(8,128)} %get-tuple-element.774, pred[]{:T(512)S(6)} %compare.8), kind=kLoop, calls=%fused_computation.10.clone.clone.1 | loop fusion | flops 6291456 | bytes 37748736 | tf_op jit(solution)/shard_map/while/body/eval_jaxpr/add | solution.py:48
  192.6 11.4 %copy.66 = f32[18,8,64,256]{3,1,2,0:T(8,128)} copy(f32[18,8,64,256]{3,2,1,0:T(8,128)S(1)} %bitcast.144) | data formatting | bytes 18874368 | tf_op jit(solution)/shard_map/while
  204.0 5.6 fusion.72
  209.6 13.7 %convolution_add_fusion.6 = f32[192,16384]{1,0:T(8,128)} fusion(f32[192,16384]{1,0:T(8,128)S(1)} %fusion.72, f32[144,16384]{1,0:T(8,128)} %bitcast.142, s32[144]{0:T(256)S(1)} %dynamic_slice.115), kind=kOutput, calls=%fused_computation.8.clone.clone.1 | convolution fusion | flops 918580224 | bytes 34603584 | tf_op jit(solution)/shard_map/while/body/eval_jaxpr/dot_general | solution.py:47
  223.3 13.8 %copy.67 = f32[24,8,64,256]{3,2,1,0:T(8,128)} copy(f32[24,8,64,256]{3,1,2,0:T(8,128)} %bitcast.143) | data formatting | bytes 25165824 | tf_op jit(solution)/shard_map/while
  237.2 14.7 %bitcast_add_fusion.6 = f32[192,64,256]{2,1,0:T(8,128)} fusion(f32[24,8,64,256]{3,2,1,0:T(8,128)} %copy.67, f32[192,64,256]{2,1,0:T(8,128)} %get-tuple-element.774, pred[]{:T(512)S(6)} %compare.8), kind=kLoop, calls=%fused_computation.10.clone.clone.1 | loop fusion | flops 6291456 | bytes 37748736 | tf_op jit(solution)/shard_map/while/body/eval_jaxpr/add | solution.py:48
  252.2 8.2 %convert_element_type.122 = bf16[192,64,256]{2,1,0:T(8,128)(2,1)} convert(f32[192,64,256]{2,1,0:T(8,128)} %get-tuple-element.375) | non-fusion elementwise | flops 3145728 | bytes 18874368 | tf_op jit(solution)/shard_map/convert_element_type | solution.py:88
  262.6 69.4 %reduce-scatter.6.cloned.1.call-done = bf16[3072,256]{1,0:T(8,128)(2,1)} async-done(((bf16[12288,256]{1,0:T(8,128)(2,1)}), bf16[3072,256]{1,0:T(8,128)(2,1)}) %reduce-scatter.6.cloned.1.call-update) | async-done | bytes 1572880 | tf_op jit(solution)/shard_map/reduce_scatter | solution.py:88
  332.0 4.7 fusion.20
  338.9 68.1 %all-gather.5.cloned.1.call-done = bf16[256,12288]{0,1:T(8,128)(2,1)} async-done(((bf16[256,3072]{0,1:T(8,128)(2,1)}), bf16[256,12288]{0,1:T(8,128)(2,1)}) %all-gather.5.cloned.1.call-update) | async-done | bytes 6291472 | tf_op jit(solution)/shard_map/all_gather | solution.py:94
  407.0 10.5 %reshape_reshape.30 = bf16[192,16384]{1,0:T(8,128)(2,1)} reshape(bf16[12288,256]{1,0:T(8,128)(2,1)} %bitcast.156) | data formatting | bytes 12582912 | tf_op jit(solution)/shard_map/while/body/eval_jaxpr/reshape;reshape | solution.py:36
  417.5 10.4 %reshape_reshape.36 = bf16[192,16384]{1,0:T(8,128)(2,1)} reshape(bf16[12288,256]{1,0:T(8,128)(2,1)} %bitcast.157) | data formatting | bytes 12582912 | tf_op jit(solution)/shard_map/while/body/eval_jaxpr/reshape;reshape | solution.py:36
  427.9 98.9 %while.46 = (s32[]{:T(128)}, f32[48,64,256]{2,1,0:T(8,128)}, s32[432]{0:T(512)S(1)}, bf16[432,64,64]{0,2,1:T(8,128)(2,1)}, s32[432]{0:T(512)S(1)}, /*index=5*/bf...) while((s32[]{:T(128)}, f32[48,64,256]{2,1,0:T(8,128)}, ...), condition=%wide.wide.region_4.0_spmd.clone, body=%wide.wide.region_3.0_spmd.clone.sunk | while | flops 1679860224 | bytes 117577552 | solution.py:27
  437.1 4.5 copy.68
  446.1 7.7 %copy.70 = f32[18,8,64,256]{3,1,2,0:T(8,128)S(1)} copy(f32[18,8,64,256]{3,2,1,0:T(8,128)S(1)} %bitcast.145) | data formatting | bytes 18874368 | tf_op jit(solution)/shard_map/while
  477.8 7.7 %copy.70 = f32[18,8,64,256]{3,1,2,0:T(8,128)S(1)} copy(f32[18,8,64,256]{3,2,1,0:T(8,128)S(1)} %bitcast.145) | data formatting | bytes 18874368 | tf_op jit(solution)/shard_map/while
  502.2 4.5 copy.68
  511.2 7.7 %copy.70 = f32[18,8,64,256]{3,1,2,0:T(8,128)S(1)} copy(f32[18,8,64,256]{3,2,1,0:T(8,128)S(1)} %bitcast.145) | data formatting | bytes 18874368 | tf_op jit(solution)/shard_map/while
  533.0 69.1 %while.44 = (s32[]{:T(128)}, bf16[432,4096]{1,0:T(8,128)(2,1)}, s32[432]{0:T(512)S(1)}, bf16[12288,256]{1,0:T(8,128)(2,1)}, s32[432]{0:T(512)S(1)}, /*index=5*/b...) while((s32[]{:T(128)}, bf16[432,4096]{1,0:T(8,128)(2,1)}, ...), condition=%wide.wide.region_7.0_spmd, body=%wide.wide.region_6.0_spmd.sunk | while | flops 480128256 | bytes 22415228 | solution.py:27
  605.3 8.5 %reduce-scatter.8.cloned.1.call-done = bf16[216,4096]{1,0:T(8,128)(2,1)} async-done(((bf16[432,4096]{1,0:T(8,128)(2,1)}), bf16[216,4096]{1,0:T(8,128)(2,1)}) %reduce-scatter.8.cloned.1.call-update) | async-done | bytes 1769488 | tf_op jit(solution)/shard_map/reduce_scatter | solution.py:131
  (208 shorter events, 197.2 us)
Async XLA Ops:
  7.2 17.8 %all-gather.3.cloned.1.call-start = ((), (), s32[]{:S(2)}) async-start(), calls=%async_computation.3 | async-start | bytes 5308416 | tf_op jit(solution)/shard_map/all_gather | solution.py:70
  7.9 324.1 %reduce-scatter.6.cloned.1.call-start = ((), (), s32[]{:S(2)}) async-start(), calls=%async_computation.4 | async-start | bytes 7864320 | tf_op jit(solution)/shard_map/reduce_scatter | solution.py:88
  9.7 21.7 %copy-start.5 = (bf16[256,3072]{0,1:T(8,128)(2,1)}, bf16[256,3072]{0,1:T(8,128)(2,1)S(1)}, u32[]{:S(2)}) copy-start(bf16[256,3072]{0,1:T(8,128)(2,1)S(1)} %copy.23) | copy-start | bytes 4718596
  11.1 20.3 %copy-start.9 = (s32[1,1,432]{2,1,0:T(1,128)S(1)}, s32[1,1,432]{2,1,0:T(1,128)}, u32[]{:S(2)}) copy-start(s32[1,1,432]{2,1,0:T(1,128)} %param.14) | copy-start | bytes 5188
  11.1 20.3 %copy-start.10 = (s32[1,1,432]{2,1,0:T(1,128)S(1)}, s32[1,1,432]{2,1,0:T(1,128)}, u32[]{:S(2)}) copy-start(s32[1,1,432]{2,1,0:T(1,128)} %param.15) | copy-start | bytes 5188
  31.4 1.5 copy-start.3
  33.0 3.6 copy-start
  91.2 11.8 %copy-start.4 = (bf16[48,16384]{1,0:T(8,128)(2,1)S(1)}, bf16[48,16384]{1,0:T(8,128)(2,1)}, u32[]{:S(2)}) copy-start(bf16[48,16384]{1,0:T(8,128)(2,1)} %copy-done.3) | copy-start | bytes 4718596 | tf_op jit(solution)/shard_map/while
  103.0 1.5 copy-start.3
  104.5 3.6 copy-start
  162.8 14.7 %copy-start.4 = (bf16[48,16384]{1,0:T(8,128)(2,1)S(1)}, bf16[48,16384]{1,0:T(8,128)(2,1)}, u32[]{:S(2)}) copy-start(bf16[48,16384]{1,0:T(8,128)(2,1)} %copy-done.3) | copy-start | bytes 4718596 | tf_op jit(solution)/shard_map/while
  177.5 1.5 copy-start.3
  179.0 3.6 copy-start
  237.2 14.7 %copy-start.4 = (bf16[48,16384]{1,0:T(8,128)(2,1)S(1)}, bf16[48,16384]{1,0:T(8,128)(2,1)}, u32[]{:S(2)}) copy-start(bf16[48,16384]{1,0:T(8,128)(2,1)} %copy-done.3) | copy-start | bytes 4718596 | tf_op jit(solution)/shard_map/while
  260.5 1.4 copy-start.8
  260.5 146.5 %all-gather.5.cloned.1.call-start = ((), (), s32[]{:S(2)}) async-start(), calls=%async_computation.5 | async-start | bytes 7864320 | tf_op jit(solution)/shard_map/all_gather | solution.py:94
  262.6 74.2 %copy-start.6 = (bf16[3072,256]{1,0:T(8,128)(2,1)S(1)}, bf16[3072,256]{1,0:T(8,128)(2,1)}, u32[]{:S(2)}) copy-start(bf16[3072,256]{1,0:T(8,128)(2,1)} %get-tuple-element.884) | copy-start | bytes 4718596
  336.7 268.5 %reduce-scatter.10.cloned.1.call-start = ((), (), s32[]{:S(2)}) async-start(), calls=%async_computation.7 | async-start | bytes 1966080 | tf_op jit(solution)/shard_map/convert_element_type | solution.py:117
  432.4 3.6 copy-start.1
  464.0 3.6 copy-start.1
  497.5 3.6 copy-start.1
  530.7 2.3 copy-start.2
  530.7 83.0 %reduce-scatter.8.cloned.1.call-start = ((), (), s32[]{:S(2)}) async-start(), calls=%async_computation.6 | async-start | bytes 5308416 | tf_op jit(solution)/shard_map/reduce_scatter | solution.py:131
  602.1 1.4 copy-start.7
Sparse Core Ops, SparseCore 0:
  9.5 15.3 all-gather.2
  260.6 71.3 reduce-scatter.5
  336.8 70.1 all-gather.4
  530.9 35.3 reduce-scatter.9
  602.3 11.4 reduce-scatter.7
where the time goes:
time: 623 us; the launch traced here: 621 us
  local copies, waits for them, and re-layouts  223 us (36%)
  waiting for transfers between devices  161 us (26%)
  matrix products  153 us (25%)
  other arithmetic  67.6 us (11%)
  between operations  14.8 us (2%)
    while x60, local copies, waits for them, and re-layouts  130 us
    reduce_scatter x1, waiting for transfers between devices, local(): lax.psum_scatter(pre_partial.astype(jnp.bfloat16), 'col', scatter_dimensi...  69.4 us
    all_gather x1, waiting for transfers between devices, local(): grad_full = lax.all_gather(grad_share, 'col', axis=1, tiled=True)  68.1 us
    dot_general x24, matrix products, pick_blocks(): jnp.dot(selector, flat, preferred_element_type=jnp.float32)  59.2 us
    add x6, other arithmetic, place_blocks(): return running + added.reshape(running.shape)  52.6 us
    dot_general x6, matrix products, place_blocks(): jnp.dot(selector.T, lower, preferred_element_type=jnp.float32)  45.2 us
    another operation x4, local copies, waits for them, and re-layouts, pick_blocks(): flat = table.reshape(table.shape[0], table.shape[1] * table.shape[2])  23.8 us
    dot_general x6, matrix products, place_blocks(): added = jnp.dot(selector.T, upper, preferred_element_type=jnp.float32)  19.5 us
  transfers between devices with their start and end apart: 5, of which 4 were waited for; matrix products, arithmetic and copies ran while one was open for 13% of the time, Pallas kernels for 0%

commit v1 on v0

--- a/solution.py
+++ b/solution.py
@@ -5,6 +5,22 @@
 
 COEFF = 0.7978845608028654
 CUBIC = 0.044715
+
+
+def gather_around(x, axis, dim):
+    ways, here, step = (lax.axis_size(axis), lax.axis_index(axis), x.shape[dim])
+    lengths = [n * ways if d == dim else n for d, n in enumerate(x.shape)]
+    full = lax.dynamic_update_slice_in_dim(jnp.zeros(lengths, x.dtype), x, here * step, axis=dim)
+    going_up = going_down = x
+    for far in range(1, ways // 2 + 1):
+        going_up = lax.ppermute(going_up, axis, [(d, (d + 1) % ways) for d in range(ways)])
+        full = lax.dynamic_update_slice_in_dim(full, going_up, (here - far) % ways * step, axis=dim)
+        if 2 * far < ways:
+            going_down = lax.ppermute(going_down, axis, [(d, (d - 1) % ways) for d in range(ways)])
+            full = lax.dynamic_update_slice_in_dim(
+                full, going_down, (here + far) % ways * step, axis=dim
+            )
+    return full
 
 
 def gelu_value(values):
@@ -91,7 +107,7 @@
     )
     activation = gelu_value(pre_share).astype(jnp.bfloat16)
     grad_share = (act_grad.astype(jnp.float32) * gelu_slope(pre_share)).astype(jnp.bfloat16)
-    grad_full = lax.all_gather(grad_share, "col", axis=1, tiled=True)
+    grad_full = gather_around(grad_share, "col", 1)
     grad_blocks = grad_full.T.reshape(out_blocks, 64, token_count)
     empty_cols = jnp.zeros((in_blocks, 64, token_count), jnp.float32)
     piece = lax.all_gather(weight_tiles, "dp", axis=2, tiled=True)

time: 623 us -> 646 us (1.037)
  waiting for transfers between devices: 161 us -> 185 us
  matrix products: 153 us -> 141 us
  local copies, waits for them, and re-layouts: 223 us -> 231 us
    ppermute x0 -> x3, waiting for transfers between devices: none -> 95.4 us  [the longest x2 65.5 us: gather_around(): lax.ppermute(going_up, axis, [(d, (d + 1) % ways) for d in range(ways)])]
    all_gather x1 -> x0, waiting for transfers between devices: 68.1 us -> none  [local(): grad_full = lax.all_gather(grad_share, 'col', axis=1, tiled=True)]
    while x60 -> x42, local copies, waits for them, and re-layouts: 130 us -> 117 us
    dot_general x3, matrix products: 13.3 us -> 4.1 us  [advance(): jnp.einsum('sik,sit->skt', group_tiles, gathered, preferred_element_type=...]
    dot_general x3, matrix products: 11.1 us -> 4.12 us  [advance(): jnp.einsum('sik,skt->sit', group_tiles, gathered, preferred_element_type=...]
    dynamic_update_slice x0 -> x3, local copies, waits for them, and re-layouts: none -> 6.58 us  [the longest x2 3.92 us: gather_around(): lax.dynamic_update_slice_in_dim(full, going_up, (here - far) % ways * ste...]
  transfers between devices with their start and end apart: 5 -> 7, of which waited for: 4 -> 6; matrix products, arithmetic and copies ran while one was open for 13% -> 13% of each run, Pallas kernels for 0% -> 0%
where the time goes in v1:
time: 646 us; the launch traced here: 644 us
  local copies, waits for them, and re-layouts  231 us (36%)
  waiting for transfers between devices  185 us (29%)
  matrix products  141 us (22%)
  other arithmetic  66.9 us (10%)
  between operations  14.8 us (2%)
    while x42, local copies, waits for them, and re-layouts  117 us
    reduce_scatter x1, waiting for transfers between devices, local(): lax.psum_scatter(pre_partial.astype(jnp.bfloat16), 'col', scatter_dimensi...  69.5 us
    ppermute x2, waiting for transfers between devices, gather_around(): lax.ppermute(going_up, axis, [(d, (d + 1) % ways) for d in range(ways)])  65.5 us
    dot_general x24, matrix products, pick_blocks(): jnp.dot(selector, flat, preferred_element_type=jnp.float32)  63.4 us
    add x6, other arithmetic, place_blocks(): return running + added.reshape(running.shape)  52.1 us
    dot_general x6, matrix products, place_blocks(): jnp.dot(selector.T, lower, preferred_element_type=jnp.float32)  44.8 us
    ppermute x1, waiting for transfers between devices, gather_around(): lax.ppermute(going_down, axis, [(d, (d - 1) % ways) for d in range(ways)])  29.9 us
    another operation x4, local copies, waits for them, and re-layouts, pick_blocks(): flat = table.reshape(table.shape[0], table.shape[1] * table.shape[2])  25.1 us
  transfers between devices with their start and end apart: 7, of which 6 were waited for; matrix products, arithmetic and copies ran while one was open for 13% of the time, Pallas kernels for 0%

profile of v1, /device:TPU:0, one launch (start us, length us, event | category | flops | bytes accessed | tf_op | source)
XLA Modules:
  0.0 644.0 jit_solution(8583693936274955034)
XLA Ops:
  12.4 12.5 %all-gather.2.cloned.1.call-done = bf16[1,1,432,4096]{3,2,1,0:T(8,128)(2,1)} async-done(((bf16[1,1,216,4096]{3,2,1,0:T(8,128)(2,1)}), bf16[1,1,432,4096]{3,2,1,0:T(8,128)(2,1)}) %all-gather.2.cloned.1.call-update) | async-done | bytes 3538960 | tf_op jit(solution)/shard_map/all_gather | solution.py:86
  25.0 6.4 %copy.24 = bf16[1,1,432,4096]{2,3,1,0:T(8,128)(2,1)} copy(bf16[1,1,432,4096]{3,2,1,0:T(8,128)(2,1)} %all-gather.2.cloned.1.call-done) | data formatting | bytes 7077888 | tf_op jit(solution)/shard_map/all_gather | solution.py:86
  31.4 215.5 %while.45 = (s32[]{:T(128)}, f32[192,64,256]{2,1,0:T(8,128)}, s32[432]{0:T(512)S(1)}, bf16[432,64,64]{0,2,1:T(8,128)(2,1)}, s32[432]{0:T(512)S(1)}, /*index=5*/b...) while((s32[]{:T(128)}, f32[192,64,256]{2,1,0:T(8,128)}, ...), condition=%wide.wide.region_1.0_spmd.clone, body=%wide.wide.region_0.0_spmd.clone.sunk | while | flops 2366436096 | bytes 174200656 | solution.py:43
  45.3 11.3 %copy.68 = f32[18,8,64,256]{3,1,2,0:T(8,128)} copy(f32[18,8,64,256]{3,2,1,0:T(8,128)S(1)} %bitcast.145) | data formatting | bytes 18874368 | tf_op jit(solution)/shard_map/while
  56.6 5.6 fusion.73
  62.3 13.6 %convolution_add_fusion.6 = f32[192,16384]{1,0:T(8,128)} fusion(f32[192,16384]{1,0:T(8,128)S(1)} %fusion.73, f32[144,16384]{1,0:T(8,128)} %bitcast.143, s32[144]{0:T(256)S(1)} %dynamic_slice.115), kind=kOutput, calls=%fused_computation.8.clone.clone.1 | convolution fusion | flops 918580224 | bytes 34603584 | tf_op jit(solution)/shard_map/while/body/eval_jaxpr/dot_general | solution.py:63
  75.8 13.8 %copy.69 = f32[24,8,64,256]{3,2,1,0:T(8,128)} copy(f32[24,8,64,256]{3,1,2,0:T(8,128)} %bitcast.144) | data formatting | bytes 25165824 | tf_op jit(solution)/shard_map/while
  89.6 11.7 %bitcast_add_fusion.6 = f32[192,64,256]{2,1,0:T(8,128)} fusion(f32[24,8,64,256]{3,2,1,0:T(8,128)} %copy.69, f32[192,64,256]{2,1,0:T(8,128)} %get-tuple-element.760, pred[]{:T(512)S(6)} %compare.11), kind=kLoop, calls=%fused_computation.10.clone.clone.1 | loop fusion | flops 6291456 | bytes 37748736 | tf_op jit(solution)/shard_map/while/body/eval_jaxpr/add | solution.py:64
  115.2 11.3 %copy.68 = f32[18,8,64,256]{3,1,2,0:T(8,128)} copy(f32[18,8,64,256]{3,2,1,0:T(8,128)S(1)} %bitcast.145) | data formatting | bytes 18874368 | tf_op jit(solution)/shard_map/while
  126.5 5.6 fusion.73
  132.1 13.6 %convolution_add_fusion.6 = f32[192,16384]{1,0:T(8,128)} fusion(f32[192,16384]{1,0:T(8,128)S(1)} %fusion.73, f32[144,16384]{1,0:T(8,128)} %bitcast.143, s32[144]{0:T(256)S(1)} %dynamic_slice.115), kind=kOutput, calls=%fused_computation.8.clone.clone.1 | convolution fusion | flops 918580224 | bytes 34603584 | tf_op jit(solution)/shard_map/while/body/eval_jaxpr/dot_general | solution.py:63
  145.7 13.8 %copy.69 = f32[24,8,64,256]{3,2,1,0:T(8,128)} copy(f32[24,8,64,256]{3,1,2,0:T(8,128)} %bitcast.144) | data formatting | bytes 25165824 | tf_op jit(solution)/shard_map/while
  159.5 14.6 %bitcast_add_fusion.6 = f32[192,64,256]{2,1,0:T(8,128)} fusion(f32[24,8,64,256]{3,2,1,0:T(8,128)} %copy.69, f32[192,64,256]{2,1,0:T(8,128)} %get-tuple-element.760, pred[]{:T(512)S(6)} %compare.11), kind=kLoop, calls=%fused_computation.10.clone.clone.1 | loop fusion | flops 6291456 | bytes 37748736 | tf_op jit(solution)/shard_map/while/body/eval_jaxpr/add | solution.py:64
  187.7 11.3 %copy.68 = f32[18,8,64,256]{3,1,2,0:T(8,128)} copy(f32[18,8,64,256]{3,2,1,0:T(8,128)S(1)} %bitcast.145) | data formatting | bytes 18874368 | tf_op jit(solution)/shard_map/while
  199.0 5.6 fusion.73
  204.6 13.6 %convolution_add_fusion.6 = f32[192,16384]{1,0:T(8,128)} fusion(f32[192,16384]{1,0:T(8,128)S(1)} %fusion.73, f32[144,16384]{1,0:T(8,128)} %bitcast.143, s32[144]{0:T(256)S(1)} %dynamic_slice.115), kind=kOutput, calls=%fused_computation.8.clone.clone.1 | convolution fusion | flops 918580224 | bytes 34603584 | tf_op jit(solution)/shard_map/while/body/eval_jaxpr/dot_general | solution.py:63
  218.2 13.8 %copy.69 = f32[24,8,64,256]{3,2,1,0:T(8,128)} copy(f32[24,8,64,256]{3,1,2,0:T(8,128)} %bitcast.144) | data formatting | bytes 25165824 | tf_op jit(solution)/shard_map/while
  232.0 14.6 %bitcast_add_fusion.6 = f32[192,64,256]{2,1,0:T(8,128)} fusion(f32[24,8,64,256]{3,2,1,0:T(8,128)} %copy.69, f32[192,64,256]{2,1,0:T(8,128)} %get-tuple-element.760, pred[]{:T(512)S(6)} %compare.11), kind=kLoop, calls=%fused_computation.10.clone.clone.1 | loop fusion | flops 6291456 | bytes 37748736 | tf_op jit(solution)/shard_map/while/body/eval_jaxpr/add | solution.py:64
  246.9 8.2 %convert_element_type.122 = bf16[192,64,256]{2,1,0:T(8,128)(2,1)} convert(f32[192,64,256]{2,1,0:T(8,128)} %get-tuple-element.375) | non-fusion elementwise | flops 3145728 | bytes 18874368 | tf_op jit(solution)/shard_map/convert_element_type | solution.py:104
  257.2 69.5 %reduce-scatter.6.cloned.1.call-done = bf16[3072,256]{1,0:T(8,128)(2,1)} async-done(((bf16[12288,256]{1,0:T(8,128)(2,1)}), bf16[3072,256]{1,0:T(8,128)(2,1)}) %reduce-scatter.6.cloned.1.call-update) | async-done | bytes 1572880 | tf_op jit(solution)/shard_map/reduce_scatter | solution.py:104
  336.0 35.5 %collective-permute-done = bf16[256,3072]{0,1:T(8,128)(2,1)S(1)} collective-permute-done((bf16[256,3072]{0,1:T(8,128)(2,1)}, bf16[256,3072]{0,1:T(8,128)(2,1)S(1)}, u32[]{:S(2)}, u32[]{:S(2)}) %collective-permute-start) | collective-permute-done | bytes 1572896 | tf_op jit(solution)/shard_map/ppermute | solution.py:16
  375.2 29.9 %collective-permute-done.1 = bf16[256,3072]{0,1:T(8,128)(2,1)} collective-permute-done((bf16[256,3072]{0,1:T(8,128)(2,1)}, bf16[256,3072]{0,1:T(8,128)(2,1)}, u32[]{:S(2)}, u32[]{:S(2)}) %collective-permute-start.1) | collective-permute-done | bytes 1572896 | tf_op jit(solution)/shard_map/ppermute | solution.py:19
  407.7 30.1 %collective-permute-done.2 = bf16[256,3072]{0,1:T(8,128)(2,1)} collective-permute-done((bf16[256,3072]{0,1:T(8,128)(2,1)S(1)}, bf16[256,3072]{0,1:T(8,128)(2,1)}, u32[]{:S(2)}, u32[]{:S(2)}) %collective-permute-start.2) | collective-permute-done | bytes 1572896 | tf_op jit(solution)/shard_map/ppermute | solution.py:16
  440.4 10.5 %reshape_reshape.36 = bf16[192,16384]{1,0:T(8,128)(2,1)} reshape(bf16[12288,256]{1,0:T(8,128)(2,1)} %bitcast.7) | data formatting | bytes 12582912 | tf_op jit(solution)/shard_map/while/body/eval_jaxpr/reshape;reshape | solution.py:52
  450.9 10.4 %reshape_reshape.30 = bf16[192,16384]{1,0:T(8,128)(2,1)} reshape(bf16[12288,256]{1,0:T(8,128)(2,1)} %bitcast.7) | data formatting | bytes 12582912 | tf_op jit(solution)/shard_map/while/body/eval_jaxpr/reshape;reshape | solution.py:52
  461.3 89.0 %while.46 = (s32[]{:T(128)}, f32[48,64,256]{2,1,0:T(8,128)}, s32[432]{0:T(512)S(1)}, bf16[432,64,64]{0,2,1:T(8,128)(2,1)}, s32[432]{0:T(512)S(1)}, /*index=5*/bf...) while((s32[]{:T(128)}, f32[48,64,256]{2,1,0:T(8,128)}, ...), condition=%wide.wide.region_4.5_spmd.clone, body=%wide.wide.region_3.4_spmd.clone.sunk | while | flops 1679860224 | bytes 108140384 | solution.py:43
  464.5 4.5 copy.70
  476.4 7.7 %copy.72 = f32[18,8,64,256]{3,1,2,0:T(8,128)S(1)} copy(f32[18,8,64,256]{3,2,1,0:T(8,128)S(1)} %bitcast.146) | data formatting | bytes 18874368 | tf_op jit(solution)/shard_map/while
  504.7 7.7 %copy.72 = f32[18,8,64,256]{3,1,2,0:T(8,128)S(1)} copy(f32[18,8,64,256]{3,2,1,0:T(8,128)S(1)} %bitcast.146) | data formatting | bytes 18874368 | tf_op jit(solution)/shard_map/while
  534.7 7.7 %copy.72 = f32[18,8,64,256]{3,1,2,0:T(8,128)S(1)} copy(f32[18,8,64,256]{3,2,1,0:T(8,128)S(1)} %bitcast.146) | data formatting | bytes 18874368 | tf_op jit(solution)/shard_map/while
  556.5 69.2 %while.44 = (s32[]{:T(128)}, bf16[432,4096]{1,0:T(8,128)(2,1)}, s32[432]{0:T(512)S(1)}, bf16[12288,256]{1,0:T(8,128)(2,1)}, s32[432]{0:T(512)S(1)}, /*index=5*/b...) while((s32[]{:T(128)}, bf16[432,4096]{1,0:T(8,128)(2,1)}, ...), condition=%wide.wide.region_7.8_spmd, body=%wide.wide.region_6.7_spmd.sunk | while | flops 480128256 | bytes 22415236 | solution.py:43
  630.0 7.3 %reduce-scatter.8.cloned.1.call-done = bf16[216,4096]{1,0:T(8,128)(2,1)} async-done(((bf16[432,4096]{1,0:T(8,128)(2,1)}), bf16[216,4096]{1,0:T(8,128)(2,1)}) %reduce-scatter.8.cloned.1.call-update) | async-done | bytes 1769488 | tf_op jit(solution)/shard_map/reduce_scatter | solution.py:147
  (200 shorter events, 206.4 us)
Async XLA Ops:
  7.2 17.8 %all-gather.2.cloned.1.call-start = ((), (), s32[]{:S(2)}) async-start(), calls=%async_computation.3 | async-start | bytes 5308416 | tf_op jit(solution)/shard_map/all_gather | solution.py:86
  7.9 318.8 %reduce-scatter.6.cloned.1.call-start = ((), (), s32[]{:S(2)}) async-start(), calls=%async_computation.4 | async-start | bytes 7864320 | tf_op jit(solution)/shard_map/reduce_scatter | solution.py:104
  9.7 21.8 %copy-start.2 = (bf16[256,3072]{0,1:T(8,128)(2,1)}, bf16[256,3072]{0,1:T(8,128)(2,1)S(1)}, u32[]{:S(2)}) copy-start(bf16[256,3072]{0,1:T(8,128)(2,1)S(1)} %copy.25) | copy-start | bytes 4718596
  12.4 19.0 %copy-start.7 = (s32[1,1,432]{2,1,0:T(1,128)S(1)}, s32[1,1,432]{2,1,0:T(1,128)}, u32[]{:S(2)}) copy-start(s32[1,1,432]{2,1,0:T(1,128)} %param.14) | copy-start | bytes 5188
  12.4 19.0 %copy-start.8 = (s32[1,1,432]{2,1,0:T(1,128)S(1)}, s32[1,1,432]{2,1,0:T(1,128)}, u32[]{:S(2)}) copy-start(s32[1,1,432]{2,1,0:T(1,128)} %param.15) | copy-start | bytes 5188
  255.1 1.4 copy-start.6
  255.1 374.8 %reduce-scatter.10.cloned.1.call-start = ((), (), s32[]{:S(2)}) async-start(), calls=%async_computation.6 | async-start | bytes 1966080 | tf_op jit(solution)/shard_map/convert_element_type | solution.py:133
  326.7 3.0 copy-start.4
  329.6 42.2 %copy-start.3 = (bf16[3072,256]{1,0:T(8,128)(2,1)S(1)}, bf16[3072,256]{1,0:T(8,128)(2,1)}, u32[]{:S(2)}) copy-start(bf16[3072,256]{1,0:T(8,128)(2,1)} %get-tuple-element.867) | copy-start | bytes 4718596
  333.0 38.4 %collective-permute-start = (bf16[256,3072]{0,1:T(8,128)(2,1)}, bf16[256,3072]{0,1:T(8,128)(2,1)S(1)}, u32[]{:S(2)}, u32[]{:S(2)}) collective-permute-start(bf16[256,3072]{0,1:T(8,128)(2,1)} %get-tuple-element.510), channel_id=1, source_target_pairs={{0,1},{1,2},{2,3},{3,0},{4,5},{5,6},{6,7},{7,4},{8,9},{9,10},{10,1... | collective-permute-start | bytes 4718600 | tf_op jit(solution)/shard_map/ppermute | solution.py:16
  334.3 70.7 %collective-permute-start.1 = (bf16[256,3072]{0,1:T(8,128)(2,1)}, bf16[256,3072]{0,1:T(8,128)(2,1)}, u32[]{:S(2)}, u32[]{:S(2)}) collective-permute-start(bf16[256,3072]{0,1:T(8,128)(2,1)} %get-tuple-element.510), channel_id=1, source_target_pairs={{0,3},{1,0},{2,1},{3,2},{4,7},{5,4},{6,5},{7,6},{8,11},{9,8},{10,9... | collective-permute-start | bytes 4718600 | tf_op jit(solution)/shard_map/ppermute | solution.py:19
  371.4 66.4 %collective-permute-start.2 = (bf16[256,3072]{0,1:T(8,128)(2,1)S(1)}, bf16[256,3072]{0,1:T(8,128)(2,1)}, u32[]{:S(2)}, u32[]{:S(2)}) collective-permute-start(bf16[256,3072]{0,1:T(8,128)(2,1)S(1)} %collective-permute-done), channel_id=1, source_target_pairs={{0,1},{1,2},{2,3},{3,0},{4,5},{5,6},{6,7},{7,4},{8,9},{9,10},{10,1... | collective-permute-start | bytes 4718600 | tf_op jit(solution)/shard_map/ppermute | solution.py:16
  473.3 1.7 copy-start
  501.7 1.7 copy-start
  531.7 1.7 copy-start
  554.2 2.3 copy-start.1
  554.2 83.0 %reduce-scatter.8.cloned.1.call-start = ((), (), s32[]{:S(2)}) async-start(), calls=%async_computation.5 | async-start | bytes 5308416 | tf_op jit(solution)/shard_map/reduce_scatter | solution.py:147
  625.7 1.4 copy-start.5
Sparse Core Ops, SparseCore 0:
  9.5 15.3 all-gather.1
  255.2 71.3 reduce-scatter.5
  554.4 35.1 reduce-scatter.9
  625.9 11.2 reduce-scatter.7
